TPU v7x, 32 devices: a whole 2x2x4 slice. The times are simulated.
32 devices in a mesh: replica: 8 (over y, x, core), tensor: 4 (over z).
Axes of the slice: x: 2, y: 2, z: 4, core: 2. Of those that a mesh axis runs over, the one named last changes fastest.
Arguments:
- queries: bfloat16 [8, 512, 2560], P('replica', None, 'tensor'), may hold values from -160 to 160
- key_rows: bfloat16 [8, 512, 2560], P('replica', None, 'tensor'), may hold values from -4 to 4
- value_rows: bfloat16 [8, 512, 2560], P('replica', None, 'tensor'), may hold values from -6 to 6
- out_grads: bfloat16 [8, 512, 1024], P('replica', 'tensor'), may hold values from -6 to 6
- inner_weights: bfloat16 [8, 20, 128, 1024], P('replica', 'tensor'), may hold values from -0.15625 to 0.15625
- adam_first: bfloat16 [8, 20, 128, 1024], P('replica', 'tensor'), may hold values from -12 to 12
- adam_second: bfloat16 [8, 20, 128, 1024], P('replica', 'tensor'), may hold values from 1 to 16
- anchor: bfloat16 [20, 128, 1024], P('tensor'), may hold values from -0.125 to 0.125
- momentum: float32 [20, 128, 1024], P('tensor', 'replica'), may hold values from -0.06 to 0.06
Outputs:
- query_grads: bfloat16 [8, 512, 2560], P('replica', None, 'tensor')
- key_grads: bfloat16 [8, 512, 2560], P('replica', None, 'tensor')
- value_grads: bfloat16 [8, 512, 2560], P('replica', None, 'tensor')
- new_first: bfloat16 [8, 20, 128, 1024], P('replica', 'tensor')
- new_second: bfloat16 [8, 20, 128, 1024], P('replica', 'tensor')
- new_anchor: bfloat16 [20, 128, 1024], P('tensor')
- new_momentum: float32 [20, 128, 1024], P('tensor', 'replica')
All inputs are finite; a program needn't handle non-finite values.
Results may differ from a plain program's by a relative error of at most 0.028.
Values may be sent and summed in bfloat16 or wider, within the bound.
A program may use at most 64 MiB of HBM per device.

v0:
```python
import math
import jax
import jax.numpy as jnp
from jax import lax
from jax.sharding import PartitionSpec as P

DH = 128
beta_first = 0.9
beta_second = 0.95
correct_first = 0.9999734386011124
correct_second = 0.994079470779666
inner_rate = 0.01
decay_rate = 0.1
epsilon = 1e-08
outer_rate = 0.7
outer_beta = 0.9


def local(
    queries,
    key_rows,
    value_rows,
    out_grads,
    inner_weights,
    adam_first,
    adam_second,
    anchor,
    momentum,
):
    length = queries.shape[1]
    inner_width = queries.shape[2]
    head_count = inner_width // DH
    model_width = out_grads.shape[2]
    score_scale = 1.0 / math.sqrt(DH)
    query_heads = queries[0].reshape(length, head_count, DH)
    key_heads = key_rows[0].reshape(length, head_count, DH)
    value_heads = value_rows[0].reshape(length, head_count, DH)
    scores = (
        jnp.einsum("qhc,khc->hqk", query_heads, key_heads, preferred_element_type=jnp.float32)
        * score_scale
    )
    probs = jax.nn.softmax(scores, axis=-1)
    probs_low = probs.astype(jnp.bfloat16)
    attention = jnp.einsum(
        "hqk,khc->qhc", probs_low, value_heads, preferred_element_type=jnp.float32
    ).astype(jnp.bfloat16)
    attention_rows = attention.reshape(length, inner_width)
    proj_rows = inner_weights[0].reshape(inner_width, model_width)
    block_rows = lax.all_gather(out_grads[0], "tensor", axis=0, tiled=True)
    product_rows = lax.dot_general(
        block_rows, proj_rows, (((1,), (1,)), ((), ())), preferred_element_type=jnp.float32
    ).astype(jnp.bfloat16)
    grad_rows = product_rows
    gradient = lax.dot_general(
        attention_rows, block_rows, (((0,), (0,)), ((), ())), preferred_element_type=jnp.float32
    )
    grad_rows, gradient = (grad_rows, gradient)
    grad_attn = grad_rows.reshape(length, head_count, DH)
    value_grads = jnp.einsum(
        "hqk,qhc->khc", probs_low, grad_attn, preferred_element_type=jnp.float32
    ).astype(jnp.bfloat16)
    grad_probs = jnp.einsum(
        "qhc,khc->hqk", grad_attn, value_heads, preferred_element_type=jnp.float32
    )
    row_dot = jnp.einsum("qhc,qhc->hq", grad_attn, attention, preferred_element_type=jnp.float32)
    grad_scores = (probs * (grad_probs - row_dot[:, :, None])).astype(jnp.bfloat16)
    query_grads = (
        jnp.einsum("hqk,khc->qhc", grad_scores, key_heads, preferred_element_type=jnp.float32)
        * score_scale
    ).astype(jnp.bfloat16)
    key_grads = (
        jnp.einsum("hqk,qhc->khc", grad_scores, query_heads, preferred_element_type=jnp.float32)
        * score_scale
    ).astype(jnp.bfloat16)
    grad_proj = gradient.reshape(head_count, DH, model_width)
    first_moment = beta_first * adam_first[0].astype(jnp.float32) + (1.0 - beta_first) * grad_proj
    second_moment = (
        beta_second * adam_second[0].astype(jnp.float32)
        + (1.0 - beta_second) * grad_proj * grad_proj
    )
    previous = inner_weights[0].astype(jnp.float32)
    stepped = previous - inner_rate * (
        first_moment / correct_first / (jnp.sqrt(second_moment / correct_second) + epsilon)
        + decay_rate * previous
    )
    anchor_wide = anchor.astype(jnp.float32)
    delta_terms = (anchor_wide - stepped).astype(jnp.bfloat16).astype(jnp.float32)
    workers = lax.axis_size("replica")
    slab = momentum.shape[1]
    portion = lax.psum_scatter(
        delta_terms.astype(jnp.bfloat16), "replica", scatter_dimension=1, tiled=True
    ).astype(jnp.float32)
    average = portion / workers
    new_momentum = outer_beta * momentum + average
    anchor_part = lax.dynamic_slice_in_dim(anchor_wide, lax.axis_index("replica") * slab, slab, 1)
    updated = (anchor_part - outer_rate * (average + outer_beta * new_momentum)).astype(
        jnp.bfloat16
    )
    new_anchor = lax.all_gather(updated, "replica", axis=1, tiled=True)
    return (
        query_grads.reshape(length, inner_width)[None],
        key_grads.reshape(length, inner_width)[None],
        value_grads.reshape(length, inner_width)[None],
        first_moment.astype(jnp.bfloat16)[None],
        second_moment.astype(jnp.bfloat16)[None],
        new_anchor,
        new_momentum,
    )


def solution(mesh):
    in_specs = (
        P("replica", None, "tensor"),
        P("replica", None, "tensor"),
        P("replica", None, "tensor"),
        P("replica", "tensor", None),
        P("replica", "tensor", None, None),
        P("replica", "tensor", None, None),
        P("replica", "tensor", None, None),
        P("tensor", None, None),
        P("tensor", "replica", None),
    )
    out_specs = (
        P("replica", None, "tensor"),
        P("replica", None, "tensor"),
        P("replica", None, "tensor"),
        P("replica", "tensor", None, None),
        P("replica", "tensor", None, None),
        P("tensor", None, None),
        P("tensor", "replica", None),
    )
    return jax.shard_map(local, mesh=mesh, in_specs=in_specs, out_specs=out_specs, check_vma=False)
```

profile of v0, /device:TPU:0, one launch (start us, length us, event | category | flops | bytes accessed | tf_op | source)
XLA Modules:
  0.0 125.8 jit_solution(16689872000383346448)
XLA Ops:
  7.2 0.7 all-gather.6.cloned.1.call-update
  8.0 1.3 %copy.32 = bf16[1,512,640]{1,2,0:T(8,128)(2,1)S(1)} copy(bf16[1,512,640]{2,1,0:T(8,128)(2,1)} %param.9) | data formatting | bytes 1310720 | tf_op args[0]
  9.3 1.6 %copy.33 = bf16[1,512,640]{1,2,0:T(8,128)(2,1)S(1)} copy(bf16[1,512,640]{2,1,0:T(8,128)(2,1)} %param.10) | data formatting | bytes 1310720 | tf_op args[1]
  10.9 1.1 copy.37
  12.0 4.1 %fusion.25 = (f32[5,512]{1,0:T(8,128)S(1)}, f32[5,512,512]{1,2,0:T(8,128)}) fusion(bf16[512,5,128]{0,2,1:T(8,128)(2,1)S(1)} %bitcast.86, bf16[512,5,128]{0,2,1:T(8,128)(2,1)S(1)} %bitcast.82), kind=kOutput, calls=%fused_computation.39 | convolution fusion | flops 339476992 | bytes 6563840 | tf_op jit(solution)/shard_map/sub | solution.py:42
  16.1 3.2 %fusion.10 = bf16[5,512,512]{1,2,0:T(8,128)(2,1)S(1)} fusion(f32[5,512,512]{1,2,0:T(8,128)} %get-tuple-element.27, f32[5,512]{1,0:T(8,128)S(1)} %get-tuple-element.26), kind=kLoop, calls=%fused_computation.16 | loop fusion | flops 2621440 | bytes 7874560 | tf_op jit(solution)/shard_map/convert_element_type | solution.py:43
  19.3 20.9 %all-gather.6.cloned.1.call-done = bf16[1,512,1024]{2,1,0:T(8,128)(2,1)} async-done(((bf16[1,128,1024]{2,1,0:T(8,128)(2,1)}), bf16[1,512,1024]{2,1,0:T(8,128)(2,1)}) %all-gather.6.cloned.1.call-update) | async-done | bytes 1048592 | tf_op jit(solution)/shard_map/all_gather | solution.py:49
  40.3 3.5 %convolution_convert_fusion = bf16[512,640]{1,0:T(8,128)(2,1)} fusion(bf16[640,1024]{1,0:T(8,128)(2,1)} %bitcast.89, bf16[1,512,1024]{2,1,0:T(8,128)(2,1)} %all-gather.6.cloned.1.call-done), kind=kOutput, calls=%fused_computation.22 | convolution fusion | flops 671416320 | bytes 3014656 | tf_op jit(solution)/shard_map/dot_general | solution.py:50
  43.8 1.3 %copy.36 = bf16[512,640]{0,1:T(8,128)(2,1)S(1)} copy(bf16[512,640]{1,0:T(8,128)(2,1)} %convolution_convert_fusion) | data formatting | bytes 1310720 | tf_op jit(solution)/shard_map/convert_element_type | solution.py:52
  45.2 1.8 %fusion.17 = (f32[5,512]{1,0:T(8,128)S(1)}, bf16[5,512,128]{1,2,0:T(8,128)(2,1)S(1)}) fusion(bf16[5,512,128]{1,2,0:T(8,128)(2,1)S(1)} %bitcast.77, bf16[512,5,128]{0,2,1:T(8,128)(2,1)} %bitcast.80, bf16[5,512,512]{1,2,0:T(8,128)(2,1)S(1)} %fusion.10), kind=kOutput, calls=%fused_computation.29 | convolution fusion | flops 337180160 | bytes 4597760 | tf_op jit(solution)/shard_map/hqk,khc->qhc/dot_general | solution.py:44
  47.4 5.9 %fusion.7 = (bf16[5,128,1024]{2,1,0:T(8,128)(2,1)}, bf16[1,5,128,1024]{3,2,1,0:T(8,128)(2,1)}, bf16[1,5,128,1024]{3,2,1,0:T(8,128)(2,1)}) fusion(bf16[1,5,128,1024]{3,2,1,0:T(8,128)(2,1)S(1)} %copy-done.7, bf16[1,5,128,1024]{3,2,1,0:T(8,128)(2,1)} %param.15, bf16[1,5,128,1024]{3,2,1,0:T(8,128)(2,1)S(1)} %copy-done.6, ...), kind=kOutput, calls=%fused_computation.11 | convolution fusion | flops 686161920 | bytes 10878976 | tf_op jit(solution)/shard_map/dot_general | solution.py:54
  53.4 3.1 %convert_element_type.82 = f32[5,128,1024]{2,1,0:T(8,128)} convert(bf16[5,128,1024]{2,1,0:T(8,128)(2,1)} %param.16) | non-fusion elementwise | flops 655360 | bytes 3932160 | tf_op jit(solution)/shard_map/convert_element_type | solution.py:86
  56.5 33.6 %reduce-scatter.2.cloned.1.call-done = bf16[5,16,1024]{2,1,0:T(8,128)(2,1)} async-done(((bf16[5,128,1024]{2,1,0:T(8,128)(2,1)}), bf16[5,16,1024]{2,1,0:T(8,128)(2,1)}) %reduce-scatter.2.cloned.1.call-update) | async-done | bytes 163856 | tf_op jit(solution)/shard_map/reduce_scatter | solution.py:90
  90.1 2.0 %subtract_convert_fusion = (bf16[5,16,1024]{2,1,0:T(8,128)(2,1)}, f32[5,16,1024]{2,1,0:T(8,128)}) fusion(bf16[5,16,1024]{2,1,0:T(8,128)(2,1)} %reduce-scatter.2.cloned.1.call-done, f32[5,128,1024]{2,1,0:T(8,128)} %convert_element_type.82, s32[]{:T(128)S(6)} %select_n.3, f32[5,16,1024]{2,1,0:T(8,128)} %param.17), kind=kLoop, calls=%fused_computation.35 | loop fusion | flops 737280 | bytes 1310724 | tf_op jit(solution)/shard_map/convert_element_type | solution.py:96
  92.1 3.7 %multiply_convert_fusion = bf16[5,512,512]{1,2,0:T(8,128)(2,1)S(1)} fusion(f32[5,512]{1,0:T(8,128)S(1)} %get-tuple-element.28, bf16[512,5,128]{0,2,1:T(8,128)(2,1)S(1)} %bitcast.78, bf16[512,5,128]{0,2,1:T(8,128)(2,1)} %bitcast.81, f32[5,512,512]{1,2,0:T(8,128)} %get-tuple-element.27, f32[5,512]{1,0:T(8,128)S(1)} %get-tuple-element.26), kind=kOutput, calls=%fused_computation.1 | convolution fusion | flops 340787200 | bytes 9195520 | tf_op jit(solution)/shard_map/qhc,khc->hqk/dot_general | solution.py:62
  95.8 1.5 %copy-done = bf16[5,512,512]{1,2,0:T(8,128)(2,1)} copy-done((bf16[5,512,512]{1,2,0:T(8,128)(2,1)}, bf16[5,512,512]{1,2,0:T(8,128)(2,1)S(1)}, u32[]{:S(2)}) %copy-start) | copy-done | bytes 2621464
  97.3 1.8 %fusion.12 = bf16[5,512,128]{1,2,0:T(8,128)(2,1)} fusion(bf16[5,512,512]{1,2,0:T(8,128)(2,1)S(1)} %multiply_convert_fusion, bf16[512,5,128]{0,2,1:T(8,128)(2,1)S(1)} %bitcast.87), kind=kOutput, calls=%fused_computation.20 | convolution fusion | flops 336199680 | bytes 3932160 | tf_op jit(solution)/shard_map/hqk,qhc->khc/dot_general | solution.py:72
  99.1 2.2 %copy.46 = bf16[1,512,640]{2,1,0:T(8,128)(2,1)} copy(bf16[1,512,640]{1,2,0:T(8,128)(2,1)} %bitcast.88) | data formatting | bytes 1310720
  101.3 3.3 %fusion.13 = bf16[5,512,128]{1,2,0:T(8,128)(2,1)} fusion(bf16[512,5,128]{0,2,1:T(8,128)(2,1)} %bitcast.83, bf16[5,512,512]{1,2,0:T(8,128)(2,1)} %copy-done), kind=kOutput, calls=%fused_computation.21 | convolution fusion | flops 336199680 | bytes 3932160 | tf_op jit(solution)/shard_map/hqk,khc->qhc/dot_general | solution.py:68
  104.6 2.2 %copy.45 = bf16[1,512,640]{2,1,0:T(8,128)(2,1)} copy(bf16[1,512,640]{1,2,0:T(8,128)(2,1)} %bitcast.84) | data formatting | bytes 1310720
  106.8 1.8 %convolution_convert_fusion.2 = bf16[5,128,512]{2,1,0:T(8,128)(2,1)} fusion(bf16[512,5,128]{0,2,1:T(8,128)(2,1)S(1)} %bitcast.79, bf16[5,512,512]{1,2,0:T(8,128)(2,1)S(1)} %fusion.10), kind=kOutput, calls=%fused_computation.24 | convolution fusion | flops 335872000 | bytes 3932160 | tf_op jit(solution)/shard_map/hqk,qhc->khc/dot_general | solution.py:59
  108.6 2.2 %copy.47 = bf16[1,512,640]{2,1,0:T(8,128)(2,1)} copy(bf16[1,512,640]{1,2,0:T(8,128)(2,1)} %bitcast.85) | data formatting | bytes 1310720
  110.7 6.0 %all-gather.4.cloned.1.call-done = bf16[5,128,1024]{2,1,0:T(8,128)(2,1)} async-done(((bf16[5,16,1024]{2,1,0:T(8,128)(2,1)}), bf16[5,128,1024]{2,1,0:T(8,128)(2,1)}) %all-gather.4.cloned.1.call-update) | async-done | bytes 1310736 | tf_op jit(solution)/shard_map/all_gather | solution.py:99
  116.7 2.5 %copy.67 = bf16[5,128,1024]{2,1,0:T(8,128)(2,1)} copy(bf16[5,128,1024]{2,1,0:T(8,128)(2,1)} %all-gather.4.cloned.1.call-done) | data formatting | bytes 2621440
  (20 shorter events, 0.7 us)
Async XLA Ops:
  7.2 3.7 %copy-start.3 = (bf16[1,512,640]{2,1,0:T(8,128)(2,1)S(1)}, bf16[1,512,640]{2,1,0:T(8,128)(2,1)}, u32[]{:S(2)}) copy-start(bf16[1,512,640]{2,1,0:T(8,128)(2,1)} %param.11) | copy-start | bytes 1966084
  7.2 33.1 %all-gather.6.cloned.1.call-start = ((), (), s32[]{:S(2)}) async-start(), calls=%async_computation.3 | async-start | bytes 1310720 | tf_op jit(solution)/shard_map/all_gather | solution.py:49
  7.9 82.2 %reduce-scatter.2.cloned.1.call-start = ((), (), s32[]{:S(2)}) async-start(), calls=%async_computation.1 | async-start | bytes 1474560 | tf_op jit(solution)/shard_map/reduce_scatter | solution.py:90
  9.3 6.8 %copy-start.4 = (bf16[1,512,640]{1,2,0:T(8,128)(2,1)}, bf16[1,512,640]{1,2,0:T(8,128)(2,1)S(1)}, u32[]{:S(2)}) copy-start(bf16[1,512,640]{1,2,0:T(8,128)(2,1)S(1)} %copy.32) | copy-start | bytes 1966084
  10.9 5.2 %copy-start.1 = (bf16[1,512,640]{1,2,0:T(8,128)(2,1)}, bf16[1,512,640]{1,2,0:T(8,128)(2,1)S(1)}, u32[]{:S(2)}) copy-start(bf16[1,512,640]{1,2,0:T(8,128)(2,1)S(1)} %copy.33) | copy-start | bytes 1966084
  45.1 1.8 %copy-start.2 = (bf16[5,128,1024]{2,1,0:T(8,128)(2,1)S(1)}, bf16[5,128,1024]{2,1,0:T(8,128)(2,1)}, u32[]{:S(2)}) copy-start(bf16[5,128,1024]{2,1,0:T(8,128)(2,1)} %param.16) | copy-start | bytes 3932164
  45.1 1.9 %copy-start.6 = (bf16[1,5,128,1024]{3,2,1,0:T(8,128)(2,1)S(1)}, bf16[1,5,128,1024]{3,2,1,0:T(8,128)(2,1)}, u32[]{:S(2)}) copy-start(bf16[1,5,128,1024]{3,2,1,0:T(8,128)(2,1)} %param.13) | copy-start | bytes 3932164
  45.1 2.3 %copy-start.7 = (bf16[1,5,128,1024]{3,2,1,0:T(8,128)(2,1)S(1)}, bf16[1,5,128,1024]{3,2,1,0:T(8,128)(2,1)}, u32[]{:S(2)}) copy-start(bf16[1,5,128,1024]{3,2,1,0:T(8,128)(2,1)} %param.14) | copy-start | bytes 3932164
  53.3 63.4 %all-gather.4.cloned.1.call-start = ((), (), s32[]{:S(2)}) async-start(), calls=%async_computation.2 | async-start | bytes 1474560 | tf_op jit(solution)/shard_map/all_gather | solution.py:99
  92.1 5.2 %copy-start.5 = (bf16[1,512,640]{1,2,0:T(8,128)(2,1)S(1)}, bf16[1,512,640]{1,2,0:T(8,128)(2,1)}, u32[]{:S(2)}) copy-start(bf16[1,512,640]{1,2,0:T(8,128)(2,1)} %copy-done.4) | copy-start | bytes 1966084
  95.8 1.5 %copy-start = (bf16[5,512,512]{1,2,0:T(8,128)(2,1)}, bf16[5,512,512]{1,2,0:T(8,128)(2,1)S(1)}, u32[]{:S(2)}) copy-start(bf16[5,512,512]{1,2,0:T(8,128)(2,1)S(1)} %multiply_convert_fusion) | copy-start | bytes 7864324
Sparse Core Ops, SparseCore 0:
  9.6 30.6 all-gather.5
  53.5 36.5 reduce-scatter.1
  92.2 24.4 all-gather.3
where the time goes:
time: 126 us
  waiting for transfers between devices  61.2 us (49%)
  matrix products  25.9 us (21%)
  local copies, waits for them, and re-layouts  16.4 us (13%)
  between operations  13.9 us (11%)
  other arithmetic  8.35 us (7%)
    reduce_scatter x1, waiting for transfers between devices, local(): lax.psum_scatter(delta_terms.astype(jnp.bfloat16), 'replica', scatter_dim...  33.6 us
    all_gather x1, waiting for transfers between devices, local(): block_rows = lax.all_gather(out_grads[0], 'tensor', axis=0, tiled=True)  20.9 us
    unnamed x23, local copies, waits for them, and re-layouts  15 us
    all_gather x1, waiting for transfers between devices, local(): new_anchor = lax.all_gather(updated, 'replica', axis=1, tiled=True)  5.99 us
    dot_general x1, matrix products, local(): lax.dot_general(attention_rows, block_rows, (((0,), (0,)), ((), ())), pre...  5.87 us
    sub x1, matrix products, local(): probs = jax.nn.softmax(scores, axis=-1)  4.12 us
    dot_general x1, matrix products, local(): jnp.einsum('qhc,khc->hqk', grad_attn, value_heads, preferred_element_type...  3.67 us
    dot_general x1, matrix products, local(): lax.dot_general(block_rows, proj_rows, (((1,), (1,)), ((), ())), preferre...  3.49 us
  transfers between devices with their start and end apart: 3, of which 3 were waited for; matrix products, arithmetic and copies ran while one was open for 25% of the time, Pallas kernels for 0%

commit v1 on v0

--- a/solution.py
+++ b/solution.py
@@ -1,3 +1,4 @@
+import functools
 import math
 import jax
 import jax.numpy as jnp
@@ -14,6 +15,24 @@
 epsilon = 1e-08
 outer_rate = 0.7
 outer_beta = 0.9
+
+
+def slots_touch(array_in, in_dim):
+    parts_n = lax.axis_size("tensor")
+    d_next = array_in
+    by_rank = [d_next]
+    src_i = 0
+    o_now = [(kk - 1, kk) for kk in range(1, parts_n)] + [(parts_n - 1, 0)]
+    while src_i < parts_n - 1:
+        d_next = lax.ppermute(d_next, axis_name="tensor", perm=o_now)
+        by_rank += [d_next]
+        src_i = src_i + 1
+    v_next = jnp.concatenate([*reversed(by_rank)], in_dim)
+    n_now = lax.axis_index("tensor")
+    return jnp.roll(v_next, (n_now + 1) * d_next.shape[in_dim], in_dim)
+
+
+check_the_sources_all = functools.partial(slots_touch, in_dim=0)
 
 
 def local(
@@ -46,7 +65,7 @@
     ).astype(jnp.bfloat16)
     attention_rows = attention.reshape(length, inner_width)
     proj_rows = inner_weights[0].reshape(inner_width, model_width)
-    block_rows = lax.all_gather(out_grads[0], "tensor", axis=0, tiled=True)
+    block_rows = check_the_sources_all(out_grads[0])
     product_rows = lax.dot_general(
         block_rows, proj_rows, (((1,), (1,)), ((), ())), preferred_element_type=jnp.float32
     ).astype(jnp.bfloat16)

time: 126 us -> 115 us (0.913)
  waiting for transfers between devices: 61.2 us -> 46.1 us
  starting transfers between devices: 0.12 us -> 3.34 us
  matrix products: 25.9 us -> 23.3 us
  local copies, waits for them, and re-layouts: 16.4 us -> 18.2 us
    all_gather x1 -> x0, waiting for transfers between devices: 20.9 us -> none  [local(): block_rows = lax.all_gather(out_grads[0], 'tensor', axis=0, tiled=True)]
    ppermute x0 -> x3, waiting for transfers between devices: none -> 14.2 us  [slots_touch(): d_next = lax.ppermute(d_next, axis_name='tensor', perm=o_now)]
    all_gather x1, waiting for transfers between devices: 5.99 us -> 0.01 us  [local(): new_anchor = lax.all_gather(updated, 'replica', axis=1, tiled=True)]
    ppermute x0 -> x3, starting transfers between devices: none -> 3.26 us  [slots_touch(): d_next = lax.ppermute(d_next, axis_name='tensor', perm=o_now)]
    dot_general x1, matrix products: 3.32 us -> 1.39 us  [local(): jnp.einsum('hqk,khc->qhc', grad_scores, key_heads, preferred_element_type...]
    dot_general x1, matrix products: 1.81 us -> 3.69 us  [local(): jnp.einsum('hqk,qhc->khc', grad_scores, query_heads, preferred_element_ty...]
    unnamed x23 -> x40, local copies, waits for them, and re-layouts: 15 us -> 16.8 us
    reduce_scatter x1, waiting for transfers between devices: 33.6 us -> 31.9 us  [local(): lax.psum_scatter(delta_terms.astype(jnp.bfloat16), 'replica', scatter_dim...]
  transfers between devices with their start and end apart: 3 -> 5, of which waited for: 3 -> 4; matrix products, arithmetic and copies ran while one was open for 25% -> 34% of each run, Pallas kernels for 0% -> 0%
where the time goes in v1:
time: 115 us
  waiting for transfers between devices  46.1 us (40%)
  matrix products  23.3 us (20%)
  local copies, waits for them, and re-layouts  18.2 us (16%)
  between operations  14.3 us (12%)
  other arithmetic  9.57 us (8%)
  starting transfers between devices  3.34 us (3%)
    reduce_scatter x1, waiting for transfers between devices, local(): lax.psum_scatter(delta_terms.astype(jnp.bfloat16), 'replica', scatter_dim...  31.9 us
    unnamed x40, local copies, waits for them, and re-layouts  16.8 us
    ppermute x3, waiting for transfers between devices, slots_touch(): d_next = lax.ppermute(d_next, axis_name='tensor', perm=o_now)  14.2 us
    dot_general x1, matrix products, local(): lax.dot_general(attention_rows, block_rows, (((0,), (0,)), ((), ())), pre...  4.46 us
    sub x1, matrix products, local(): probs = jax.nn.softmax(scores, axis=-1)  4.13 us
    dot_general x1, matrix products, local(): jnp.einsum('qhc,khc->hqk', grad_attn, value_heads, preferred_element_type...  3.79 us
    dot_general x1, matrix products, local(): jnp.einsum('hqk,qhc->khc', grad_scores, query_heads, preferred_element_ty...  3.69 us
    dot_general x1, matrix products, local(): lax.dot_general(block_rows, proj_rows, (((1,), (1,)), ((), ())), preferre...  3.5 us
  transfers between devices with their start and end apart: 5, of which 4 were waited for; matrix products, arithmetic and copies ran while one was open for 34% of the time, Pallas kernels for 0%

profile of v1, /device:TPU:0, one launch (start us, length us, event | category | flops | bytes accessed | tf_op | source)
XLA Modules:
  0.0 114.8 jit_solution(6037143701952601958)
XLA Ops:
  7.2 3.1 %collective-permute-start = (bf16[128,1024]{1,0:T(8,128)(2,1)}, bf16[128,1024]{1,0:T(8,128)(2,1)S(1)}, u32[]{:S(2)}, u32[]{:S(2)}) collective-permute-start(bf16[128,1024]{1,0:T(8,128)(2,1)} %bitcast.86), channel_id=1, source_target_pairs={{0,1},{1,2},{2,3},{3,0},{4,5},{5,6},{6,7},{7,4},{8,9},{9,10},{10,1... | collective-permute-start | bytes 786440 | tf_op jit(solution)/shard_map/ppermute | solution.py:27
  10.3 1.3 %copy.33 = bf16[1,512,640]{1,2,0:T(8,128)(2,1)S(1)} copy(bf16[1,512,640]{2,1,0:T(8,128)(2,1)} %param.10) | data formatting | bytes 1310720 | tf_op args[1]
  11.7 1.6 %copy.32 = bf16[1,512,640]{1,2,0:T(8,128)(2,1)S(1)} copy(bf16[1,512,640]{2,1,0:T(8,128)(2,1)} %param.9) | data formatting | bytes 1310720 | tf_op args[0]
  13.2 4.1 %fusion.28 = (f32[5,512]{1,0:T(8,128)S(1)}, f32[5,512,512]{1,2,0:T(8,128)}) fusion(bf16[512,5,128]{0,2,1:T(8,128)(2,1)S(1)} %bitcast.87, bf16[512,5,128]{0,2,1:T(8,128)(2,1)S(1)} %bitcast.80), kind=kOutput, calls=%fused_computation.50 | convolution fusion | flops 339476992 | bytes 6563840 | tf_op jit(solution)/shard_map/sub | solution.py:61
  17.4 1.5 %collective-permute-done = bf16[128,1024]{1,0:T(8,128)(2,1)S(1)} collective-permute-done((bf16[128,1024]{1,0:T(8,128)(2,1)}, bf16[128,1024]{1,0:T(8,128)(2,1)S(1)}, u32[]{:S(2)}, u32[]{:S(2)}) %collective-permute-start) | collective-permute-done | bytes 262176 | tf_op jit(solution)/shard_map/ppermute | solution.py:27
  19.0 3.2 %fusion.10 = bf16[5,512,512]{1,2,0:T(8,128)(2,1)S(1)} fusion(f32[5,512,512]{1,2,0:T(8,128)} %get-tuple-element.27, f32[5,512]{1,0:T(8,128)S(1)} %get-tuple-element.26), kind=kLoop, calls=%fused_computation.16 | loop fusion | flops 2621440 | bytes 7874560 | tf_op jit(solution)/shard_map/convert_element_type | solution.py:62
  22.3 1.3 %copy.37 = bf16[1,512,640]{1,2,0:T(8,128)(2,1)S(1)} copy(bf16[1,512,640]{2,1,0:T(8,128)(2,1)} %param.11) | data formatting | bytes 1310720 | tf_op args[2]
  23.6 4.6 %collective-permute-done.1 = bf16[128,1024]{1,0:T(8,128)(2,1)} collective-permute-done((bf16[128,1024]{1,0:T(8,128)(2,1)S(1)}, bf16[128,1024]{1,0:T(8,128)(2,1)}, u32[]{:S(2)}, u32[]{:S(2)}) %collective-permute-start.1) | collective-permute-done | bytes 262176 | tf_op jit(solution)/shard_map/ppermute | solution.py:27
  28.8 8.1 %collective-permute-done.2 = bf16[128,1024]{1,0:T(8,128)(2,1)S(1)} collective-permute-done((bf16[128,1024]{1,0:T(8,128)(2,1)}, bf16[128,1024]{1,0:T(8,128)(2,1)S(1)}, u32[]{:S(2)}, u32[]{:S(2)}) %collective-permute-start.2) | collective-permute-done | bytes 262176 | tf_op jit(solution)/shard_map/ppermute | solution.py:27
  39.0 4.5 %fusion.7 = (bf16[5,128,1024]{2,1,0:T(8,128)(2,1)}, bf16[1,5,128,1024]{3,2,1,0:T(8,128)(2,1)}, bf16[1,5,128,1024]{3,2,1,0:T(8,128)(2,1)}) fusion(bf16[1,5,128,1024]{3,2,1,0:T(8,128)(2,1)S(1)} %copy-done.10, bf16[1,5,128,1024]{3,2,1,0:T(8,128)(2,1)S(1)} %copy-done.11, bf16[1,5,128,1024]{3,2,1,0:T(8,128)(2,1)S(1)} %copy-done.12, ...), kind=kOutput, calls=%fused_computation.11 | convolution fusion | flops 686161920 | bytes 10878980 | tf_op jit(solution)/shard_map/dot_general | solution.py:73
  43.6 3.1 %convert_element_type.82 = f32[5,128,1024]{2,1,0:T(8,128)} convert(bf16[5,128,1024]{2,1,0:T(8,128)(2,1)} %param.16) | non-fusion elementwise | flops 655360 | bytes 3932160 | tf_op jit(solution)/shard_map/convert_element_type | solution.py:105
  46.7 31.9 %reduce-scatter.2.cloned.1.call-done = bf16[5,16,1024]{2,1,0:T(8,128)(2,1)} async-done(((bf16[5,128,1024]{2,1,0:T(8,128)(2,1)}), bf16[5,16,1024]{2,1,0:T(8,128)(2,1)}) %reduce-scatter.2.cloned.1.call-update) | async-done | bytes 163856 | tf_op jit(solution)/shard_map/reduce_scatter | solution.py:109
  78.6 1.9 %subtract_convert_fusion = (bf16[5,16,1024]{2,1,0:T(8,128)(2,1)}, f32[5,16,1024]{2,1,0:T(8,128)}) fusion(bf16[5,16,1024]{2,1,0:T(8,128)(2,1)} %reduce-scatter.2.cloned.1.call-done, f32[5,128,1024]{2,1,0:T(8,128)} %convert_element_type.82, s32[]{:T(128)S(6)} %select_n.18, f32[5,16,1024]{2,1,0:T(8,128)S(1)} %copy-done.8), kind=kLoop, calls=%fused_computation.36 | loop fusion | flops 737280 | bytes 1310724 | tf_op jit(solution)/shard_map/convert_element_type | solution.py:115
  80.6 3.5 %convolution_convert_fusion = bf16[512,640]{1,0:T(8,128)(2,1)} fusion(bf16[640,1024]{1,0:T(8,128)(2,1)} %bitcast.90, bf16[1024,1024]{1,0:T(8,128)(2,1)} %copy-done.9, s32[]{:T(128)S(6)} %select_n.17), kind=kOutput, calls=%fused_computation.22 | convolution fusion | flops 671416320 | bytes 3014660 | tf_op jit(solution)/shard_map/dot_general | solution.py:69
  84.1 1.3 %copy.36 = bf16[512,640]{0,1:T(8,128)(2,1)S(1)} copy(bf16[512,640]{1,0:T(8,128)(2,1)} %convolution_convert_fusion) | data formatting | bytes 1310720 | tf_op jit(solution)/shard_map/convert_element_type | solution.py:71
  86.7 3.8 %multiply_convert_fusion = bf16[5,512,512]{1,2,0:T(8,128)(2,1)S(1)} fusion(f32[5,512]{1,0:T(8,128)S(1)} %fusion.17, bf16[512,5,128]{0,2,1:T(8,128)(2,1)S(1)} %bitcast.78, bf16[512,5,128]{0,2,1:T(8,128)(2,1)} %bitcast.83, f32[5,512,512]{1,2,0:T(8,128)} %get-tuple-element.27, f32[5,512]{1,0:T(8,128)S(1)} %get-tuple-element.26), kind=kOutput, calls=%fused_computation.1 | convolution fusion | flops 340787200 | bytes 9195520 | tf_op jit(solution)/shard_map/qhc,khc->hqk/dot_general | solution.py:81
  90.5 1.5 %copy-done = bf16[5,512,512]{1,2,0:T(8,128)(2,1)} copy-done((bf16[5,512,512]{1,2,0:T(8,128)(2,1)}, bf16[5,512,512]{1,2,0:T(8,128)(2,1)S(1)}, u32[]{:S(2)}) %copy-start) | copy-done | bytes 2621464
  92.0 1.4 %fusion.13 = bf16[5,512,128]{1,2,0:T(8,128)(2,1)} fusion(bf16[512,5,128]{0,2,1:T(8,128)(2,1)S(1)} %bitcast.81, bf16[5,512,512]{1,2,0:T(8,128)(2,1)S(1)} %multiply_convert_fusion), kind=kOutput, calls=%fused_computation.21 | convolution fusion | flops 336199680 | bytes 3932160 | tf_op jit(solution)/shard_map/hqk,khc->qhc/dot_general | solution.py:87
  93.4 2.2 %copy.45 = bf16[1,512,640]{2,1,0:T(8,128)(2,1)} copy(bf16[1,512,640]{1,2,0:T(8,128)(2,1)} %bitcast.85) | data formatting | bytes 1310720
  95.6 3.7 %fusion.12 = bf16[5,512,128]{1,2,0:T(8,128)(2,1)} fusion(bf16[5,512,512]{1,2,0:T(8,128)(2,1)} %copy-done, bf16[512,5,128]{0,2,1:T(8,128)(2,1)} %bitcast.88), kind=kOutput, calls=%fused_computation.20 | convolution fusion | flops 336199680 | bytes 3932160 | tf_op jit(solution)/shard_map/hqk,qhc->khc/dot_general | solution.py:91
  99.3 2.2 %copy.46 = bf16[1,512,640]{2,1,0:T(8,128)(2,1)} copy(bf16[1,512,640]{1,2,0:T(8,128)(2,1)} %bitcast.89) | data formatting | bytes 1310720
  101.5 1.8 %convolution_convert_fusion.2 = bf16[5,128,512]{2,1,0:T(8,128)(2,1)} fusion(bf16[512,5,128]{0,2,1:T(8,128)(2,1)S(1)} %bitcast.79, bf16[5,512,512]{1,2,0:T(8,128)(2,1)S(1)} %fusion.10), kind=kOutput, calls=%fused_computation.24 | convolution fusion | flops 335872000 | bytes 3932160 | tf_op jit(solution)/shard_map/hqk,qhc->khc/dot_general | solution.py:78
  103.3 2.2 %copy.47 = bf16[1,512,640]{2,1,0:T(8,128)(2,1)} copy(bf16[1,512,640]{1,2,0:T(8,128)(2,1)} %bitcast.84) | data formatting | bytes 1310720
  105.4 2.5 %copy.74 = bf16[5,128,1024]{2,1,0:T(8,128)(2,1)} copy(bf16[5,128,1024]{2,1,0:T(8,128)(2,1)} %all-gather.2.cloned.1.call-done) | data formatting | bytes 2621440
  (42 shorter events, 4.2 us)
Async XLA Ops:
  7.2 71.5 %reduce-scatter.2.cloned.1.call-start = ((), (), s32[]{:S(2)}) async-start(), calls=%async_computation.1 | async-start | bytes 1474560 | tf_op jit(solution)/shard_map/reduce_scatter | solution.py:109
  7.2 11.6 %collective-permute-start = (bf16[128,1024]{1,0:T(8,128)(2,1)}, bf16[128,1024]{1,0:T(8,128)(2,1)S(1)}, u32[]{:S(2)}, u32[]{:S(2)}) collective-permute-start(bf16[128,1024]{1,0:T(8,128)(2,1)} %bitcast.86), channel_id=1, source_target_pairs={{0,1},{1,2},{2,3},{3,0},{4,5},{5,6},{6,7},{7,4},{8,9},{9,10},{10,1... | collective-permute-start | bytes 786440 | tf_op jit(solution)/shard_map/ppermute | solution.py:27
  11.7 5.7 %copy-start.1 = (bf16[1,512,640]{1,2,0:T(8,128)(2,1)}, bf16[1,512,640]{1,2,0:T(8,128)(2,1)S(1)}, u32[]{:S(2)}) copy-start(bf16[1,512,640]{1,2,0:T(8,128)(2,1)S(1)} %copy.33) | copy-start | bytes 1966084
  13.2 4.1 %copy-start.7 = (bf16[1,512,640]{1,2,0:T(8,128)(2,1)}, bf16[1,512,640]{1,2,0:T(8,128)(2,1)S(1)}, u32[]{:S(2)}) copy-start(bf16[1,512,640]{1,2,0:T(8,128)(2,1)S(1)} %copy.32) | copy-start | bytes 1966084
  18.9 9.4 %collective-permute-start.1 = (bf16[128,1024]{1,0:T(8,128)(2,1)S(1)}, bf16[128,1024]{1,0:T(8,128)(2,1)}, u32[]{:S(2)}, u32[]{:S(2)}) collective-permute-start(bf16[128,1024]{1,0:T(8,128)(2,1)S(1)} %collective-permute-done), channel_id=1, source_target_pairs={{0,1},{1,2},{2,3},{3,0},{4,5},{5,6},{6,7},{7,4},{8,9},{9,10},{10,1... | collective-permute-start | bytes 786440 | tf_op jit(solution)/shard_map/ppermute | solution.py:27
  23.6 14.3 %copy-start.3 = (bf16[1,512,640]{1,2,0:T(8,128)(2,1)}, bf16[1,512,640]{1,2,0:T(8,128)(2,1)S(1)}, u32[]{:S(2)}) copy-start(bf16[1,512,640]{1,2,0:T(8,128)(2,1)S(1)} %copy.37) | copy-start | bytes 1966084
  28.2 8.6 %collective-permute-start.2 = (bf16[128,1024]{1,0:T(8,128)(2,1)}, bf16[128,1024]{1,0:T(8,128)(2,1)S(1)}, u32[]{:S(2)}, u32[]{:S(2)}) collective-permute-start(bf16[128,1024]{1,0:T(8,128)(2,1)} %collective-permute-done.1), channel_id=1, source_target_pairs={{0,1},{1,2},{2,3},{3,0},{4,5},{5,6},{6,7},{7,4},{8,9},{9,10},{10,1... | collective-permute-start | bytes 786440 | tf_op jit(solution)/shard_map/ppermute | solution.py:27
  28.2 9.7 %copy-start.6 = (bf16[1,128,1024]{2,1,0:T(8,128)(2,1)S(1)}, bf16[1,128,1024]{2,1,0:T(8,128)(2,1)}, u32[]{:S(2)}) copy-start(bf16[1,128,1024]{2,1,0:T(8,128)(2,1)} %param.12) | copy-start | bytes 786436
  28.2 10.7 %copy-start.12 = (bf16[1,5,128,1024]{3,2,1,0:T(8,128)(2,1)S(1)}, bf16[1,5,128,1024]{3,2,1,0:T(8,128)(2,1)}, u32[]{:S(2)}) copy-start(bf16[1,5,128,1024]{3,2,1,0:T(8,128)(2,1)} %param.13) | copy-start | bytes 3932164
  28.8 14.7 %copy-start.4 = (bf16[5,512,128]{1,2,0:T(8,128)(2,1)}, bf16[5,512,128]{1,2,0:T(8,128)(2,1)S(1)}, u32[]{:S(2)}) copy-start(bf16[5,512,128]{1,2,0:T(8,128)(2,1)S(1)} %convolution_convert_fusion.1) | copy-start | bytes 1966084
  28.8 10.2 %copy-start.5 = (bf16[5,128,1024]{2,1,0:T(8,128)(2,1)S(1)}, bf16[5,128,1024]{2,1,0:T(8,128)(2,1)}, u32[]{:S(2)}) copy-start(bf16[5,128,1024]{2,1,0:T(8,128)(2,1)} %param.16) | copy-start | bytes 3932164
  28.8 10.2 %copy-start.10 = (bf16[1,5,128,1024]{3,2,1,0:T(8,128)(2,1)S(1)}, bf16[1,5,128,1024]{3,2,1,0:T(8,128)(2,1)}, u32[]{:S(2)}) copy-start(bf16[1,5,128,1024]{3,2,1,0:T(8,128)(2,1)} %param.14) | copy-start | bytes 3932164
  28.8 10.2 %copy-start.11 = (bf16[1,5,128,1024]{3,2,1,0:T(8,128)(2,1)S(1)}, bf16[1,5,128,1024]{3,2,1,0:T(8,128)(2,1)}, u32[]{:S(2)}) copy-start(bf16[1,5,128,1024]{3,2,1,0:T(8,128)(2,1)} %param.15) | copy-start | bytes 3932164
  39.0 4.5 %copy-start.9 = (bf16[1024,1024]{1,0:T(8,128)(2,1)}, bf16[1024,1024]{1,0:T(8,128)(2,1)S(1)}, u32[]{:S(2)}) copy-start(bf16[1024,1024]{1,0:T(8,128)(2,1)S(1)} %constant_dynamic-update-slice_fusion) | copy-start | bytes 6291460
  43.5 35.2 %copy-start.8 = (f32[5,16,1024]{2,1,0:T(8,128)S(1)}, f32[5,16,1024]{2,1,0:T(8,128)}, u32[]{:S(2)}) copy-start(f32[5,16,1024]{2,1,0:T(8,128)} %param.17) | copy-start | bytes 983044
  43.5 61.9 %all-gather.2.cloned.1.call-start = ((), (), s32[]{:S(2)}) async-start(), calls=%async_computation.2 | async-start | bytes 1474560 | tf_op jit(solution)/shard_map/all_gather | solution.py:118
  86.7 5.3 %copy-start.2 = (bf16[1,512,640]{1,2,0:T(8,128)(2,1)S(1)}, bf16[1,512,640]{1,2,0:T(8,128)(2,1)}, u32[]{:S(2)}) copy-start(bf16[1,512,640]{1,2,0:T(8,128)(2,1)} %copy-done.1) | copy-start | bytes 1966084
  90.5 1.5 %copy-start = (bf16[5,512,512]{1,2,0:T(8,128)(2,1)}, bf16[5,512,512]{1,2,0:T(8,128)(2,1)S(1)}, u32[]{:S(2)}) copy-start(bf16[5,512,512]{1,2,0:T(8,128)(2,1)S(1)} %multiply_convert_fusion) | copy-start | bytes 7864324
Sparse Core Ops, SparseCore 0:
  43.6 34.9 reduce-scatter.1
  80.7 24.4 all-gather.1
